TPU v7x, 32 devices: a whole 2x2x4 slice. The times are simulated.
32 devices in a mesh: parts: 16 (over z, y, core), mp: 2 (over x).
Axes of the slice: x: 2, y: 2, z: 4, core: 2. Of those that a mesh axis runs over, the one named last changes fastest.
Arguments:
- feats: bfloat16 [2048, 1024], P('parts', 'mp'), may hold values from -6 to 6
- adj_local: bfloat16 [2048, 128], P('parts'), may hold values from -0.5 to 0.5
- adj_halo: bfloat16 [2048, 128], P('parts'), may hold values from -0.5 to 0.5
- w_graph: bfloat16 [1024, 1024], P(None, 'mp'), may hold values from -0.1875 to 0.1875
- w_query: bfloat16 [1024, 1024], P(None, 'mp'), may hold values from -0.1875 to 0.1875
- w_key: bfloat16 [1024, 1024], P(None, 'mp'), may hold values from -0.1875 to 0.1875
- w_value: bfloat16 [1024, 1024], P(None, 'mp'), may hold values from -0.1875 to 0.1875
- send_rows: int32 [16, 16, 8], P('parts'), may hold values from 0 to 127
- send_count: int32 [16, 16], P('parts'), may hold values from 0 to 8
- live: int32 [16], P('parts'), may hold values from 64 to 128
Outputs:
- attended: float32 [2048, 1024], P('parts', 'mp')
- key_summary: float32 [1024, 1024], P('mp')
All inputs are finite; a program needn't handle non-finite values.
Results may differ from a plain program's by a relative error of at most 0.0029.
The roundings to bfloat16 on the way count: a program that leaves them out, or rounds other values in their place, can miss the bound.
Values may be sent and summed in bfloat16 or wider, within the bound.
A program may use at most 64 MiB of HBM per device.

v0:
```python
import math

import jax
import jax.numpy as jnp
from jax import lax
from jax.sharding import PartitionSpec as P


def local(
    feats, adj_local, adj_halo, w_graph, w_query, w_key, w_value, send_rows, send_count, live
):
    row_count, col_count = feats.shape
    slot_count = send_rows.shape[2]
    picked = feats[send_rows[0]]
    slot_live = jnp.arange(slot_count, dtype=jnp.int32)[None, :] < send_count[0][:, None]
    outgoing = jnp.where(slot_live[:, :, None], picked, jnp.zeros((), jnp.bfloat16))
    incoming = lax.all_to_all(outgoing, "parts", split_axis=0, concat_axis=0, tiled=True)
    halo_rows = incoming.reshape(-1, col_count)
    summed = jnp.dot(adj_local, feats, preferred_element_type=jnp.float32)
    summed = summed + jnp.dot(adj_halo, halo_rows, preferred_element_type=jnp.float32)
    convolved = summed.astype(jnp.bfloat16)
    out_cols = w_graph.shape[1]
    empty = jnp.zeros((row_count, out_cols), jnp.float32)
    weight_rows = w_graph
    projected = jnp.dot(
        lax.all_gather(convolved, "mp", axis=1, tiled=True),
        weight_rows,
        preferred_element_type=jnp.float32,
    )
    hidden = jax.nn.gelu(projected, approximate=False).astype(jnp.bfloat16)
    totals = (empty, empty, empty)
    portion = lax.all_gather(hidden, "mp", axis=1, tiled=True)
    outputs = []
    for running, weight in zip(totals, (w_query, w_key, w_value)):
        weight_rows = weight
        outputs.append(jnp.dot(portion, weight_rows, preferred_element_type=jnp.float32))
    queries, keys_raw, values_wide = tuple(outputs)
    live_mask = jnp.arange(row_count, dtype=jnp.int32)[:, None] < live[0]
    query_feat = jnp.where(live_mask, jax.nn.elu(queries) + 1.0, 0.0).astype(jnp.bfloat16)
    key_feat = jnp.where(live_mask, jax.nn.elu(keys_raw) + 1.0, 0.0).astype(jnp.bfloat16)
    values = values_wide.astype(jnp.bfloat16)
    key_values = lax.dot_general(
        key_feat,
        lax.all_gather(values, "mp", axis=1, tiled=True),
        (((0,), (0,)), ((), ())),
        preferred_element_type=jnp.float32,
    )
    query_wide = query_feat.astype(jnp.float32)
    key_wide = key_feat.astype(jnp.float32)
    key_total = jnp.sum(key_wide, axis=0)
    sq_pair = jnp.stack([jnp.sum(query_wide * query_wide), jnp.sum(key_wide * key_wide)])
    key_values, key_total, sq_pair = lax.psum((key_values, key_total, sq_pair), "parts")
    key_summary = key_values / math.sqrt(lax.axis_size("parts") * row_count)
    numer_part = jnp.dot(
        query_feat, key_values.astype(jnp.bfloat16), preferred_element_type=jnp.float32
    )
    denom_part = jnp.dot(query_wide, key_total, precision=lax.Precision.HIGHEST)
    numerator = lax.psum_scatter(
        numer_part.astype(jnp.bfloat16), "mp", scatter_dimension=1, tiled=True
    ).astype(jnp.float32)
    denominator, sq_pair = lax.psum((denom_part, sq_pair), "mp")
    inverse = lax.rsqrt(sq_pair[0]) * lax.rsqrt(sq_pair[1])
    result = (values.astype(jnp.float32) + numerator * inverse) / (1.0 + denominator * inverse)[
        :, None
    ]
    return (jnp.where(live_mask, result, 0.0), key_summary)


def solution(mesh):
    return jax.shard_map(
        local,
        mesh=mesh,
        in_specs=(
            P("parts", "mp"),
            P("parts", None),
            P("parts", None),
            P(None, "mp"),
            P(None, "mp"),
            P(None, "mp"),
            P(None, "mp"),
            P("parts", None, None),
            P("parts", None),
            P("parts"),
        ),
        out_specs=(P("parts", "mp"), P("mp", None)),
        check_vma=False,
    )
```

profile of v0, /device:TPU:0, one launch (start us, length us, event | category | flops | bytes accessed | tf_op | source)
XLA Modules:
  0.0 168.6 jit_solution(5325832999500448045)
XLA Ops:
  7.2 0.0 copy-start
  7.2 0.0 copy-start.1
  7.2 0.0 copy-start.5
  7.2 0.0 copy-start.6
  7.2 0.8 compare_select_fusion.4
  8.1 0.1 copy.13
  8.1 0.1 reshape.71
  8.2 0.7 iota_compare_fusion
  9.0 1.8 %gather_fusion = bf16[128,512]{1,0:T(8,128)(2,1)S(1)} fusion(bf16[128,512]{1,0:T(8,128)(2,1)} %param.10, s32[1024]{0:T(1024)S(1)} %pad_clamp_fusion), kind=kCustom, calls=%fused_computation | custom fusion | bytes 262656 | tf_op jit(solution)/shard_map/gather | solution.py:14
  10.8 0.7 bitcast_select_fusion
  11.5 7.4 %all-to-all-start = ((bf16[16,8,512]{2,1,0:T(8,128)(2,1)}), bf16[16,8,512]{2,1,0:T(8,128)(2,1)S(1)}, u32[]{:S(2)}, u32[]{:S(2)}) async-start(bf16[16,8,512]{2,1,0:T(8,128)(2,1)} %bitcast_select_fusion), calls=%async_computation | async-start | bytes 262144 | tf_op jit(solution)/shard_map/all_to_all | solution.py:17
  18.9 0.0 all-reduce.4.cloned.1.call-start
  19.6 7.2 %all-to-all-done = bf16[16,8,512]{2,1,0:T(8,128)(2,1)S(1)} async-done(((bf16[16,8,512]{2,1,0:T(8,128)(2,1)}), bf16[16,8,512]{2,1,0:T(8,128)(2,1)S(1)}, u32[]{:S(2)}, u32[]{:S(2)}) %all-to-all-start) | async-done | bytes 131104 | tf_op jit(solution)/shard_map/all_to_all | solution.py:17
  26.8 0.9 convolution_bitcast_fusion
  27.8 0.0 copy-done.1
  27.8 0.0 copy-done.5
  27.8 0.2 fusion
  28.0 5.6 %all_gather.9 = bf16[128,1024]{1,0:T(8,128)(2,1)S(1)} all-gather(bf16[128,512]{1,0:T(8,128)(2,1)S(1)} %fusion), channel_id=1, replica_groups=mesh['parts'=16,'mp'=2] {'mp'}, dimensions={1}, use_global_device_ids=true | all-gather | bytes 393216 | tf_op jit(solution)/shard_map/all_gather | solution.py:26
  33.6 0.0 copy-done.6
  33.6 0.0 copy-start.3
  33.6 0.9 fusion.5
  34.5 0.0 copy-start.4
  34.5 5.8 %all_gather.10 = bf16[128,1024]{1,0:T(8,128)(2,1)S(1)} all-gather(bf16[128,512]{1,0:T(8,128)(2,1)S(1)} %fusion.5), channel_id=1, replica_groups=mesh['parts'=16,'mp'=2] {'mp'}, dimensions={1}, use_global_device_ids=true | all-gather | bytes 393216 | tf_op jit(solution)/shard_map/all_gather | solution.py:32
  40.2 0.0 copy-done.3
  40.2 0.3 fusion.25
  40.5 0.0 copy-done.4
  40.6 0.3 convolution_convert_fusion.1
  40.9 5.6 %all_gather.11 = bf16[128,1024]{1,0:T(8,128)(2,1)S(1)} all-gather(bf16[128,512]{1,0:T(8,128)(2,1)S(1)} %convolution_convert_fusion.1), channel_id=1, replica_groups=mesh['parts'=16,'mp'=2] {'mp'}, dimensions={1}, use_global_device_ids=true | all-gather | bytes 393216 | tf_op jit(solution)/shard_map/all_gather | solution.py:44
  46.5 0.0 copy-done
  46.5 1.1 fusion.2
  47.6 1.8 %fusion.26 = f32[512,1024]{1,0:T(8,128)} fusion(bf16[128,512]{1,0:T(8,128)(2,1)S(1)} %get-tuple-element.10, bf16[128,1024]{1,0:T(8,128)(2,1)S(1)} %all_gather.11), kind=kOutput, calls=%fused_computation.55 | convolution fusion | flops 134217728 | bytes 2490368 | tf_op jit(solution)/shard_map/dot_general | solution.py:42
  49.4 0.0 all-reduce.4.cloned.1.call-update
  49.4 0.0 reduce-scatter.2.cloned.1.call-start
  49.5 1.3 pad_maximum_fusion
  50.8 29.8 %all-reduce = (f32[512]{0:T(512)S(1)}, f32[2]{0:T(128)S(1)}) all-reduce(f32[512]{0:T(512)S(1)} %get-tuple-element.3, f32[2]{0:T(128)S(1)} %pad_maximum_fusion), channel_id=1, replica_groups=mesh['parts'=16,'mp'=2] {'parts'}, use_global_device_ids=true, to_apply=%region_7.8 | all-reduce | flops 514 | bytes 4112 | tf_op jit(solution)/shard_map/psum | solution.py:52
  80.6 0.1 convolution_bitcast_fusion.1
  80.7 5.0 %all-reduce.1 = (f32[128]{0:T(128)S(1)}, f32[2]{0:T(128)S(1)}) all-reduce(f32[128]{0:T(128)S(1)} %convolution_bitcast_fusion.1, f32[2]{0:T(128)S(1)} %get-tuple-element.5), channel_id=1, replica_groups=mesh['parts'=16,'mp'=2] {'mp'}, use_global_device_ids=true, to_apply=%region_8.9 | all-reduce | flops 130 | bytes 1040 | tf_op jit(solution)/shard_map/psum | solution.py:61
  85.7 0.6 fusion.24
  87.6 58.4 %all-reduce.4.cloned.1.call-done = f32[512,1024]{1,0:T(8,128)} async-done(((f32[512,1024]{1,0:T(8,128)}), f32[512,1024]{1,0:T(8,128)}) %all-reduce.4.cloned.1.call-update) | async-done | bytes 2097168 | tf_op jit(solution)/shard_map/psum | solution.py:52
  146.1 0.0 copy-start.2
  146.1 2.8 %convolution_convert_fusion = bf16[128,1024]{1,0:T(8,128)(2,1)} fusion(bf16[128,512]{1,0:T(8,128)(2,1)S(1)} %get-tuple-element.14, f32[512,1024]{1,0:T(8,128)} %all-reduce.4.cloned.1.call-done), kind=kOutput, calls=%fused_computation.1 | convolution fusion | flops 134873088 | bytes 2490368 | tf_op jit(solution)/shard_map/dot_general | solution.py:54
  148.8 0.0 reduce-scatter.2.cloned.1.call-update
  148.9 0.0 copy-done.2
  148.9 1.5 broadcast_multiply_fusion
  150.4 9.6 %reduce-scatter.2.cloned.1.call-done = bf16[128,512]{1,0:T(8,128)(2,1)} async-done(((bf16[128,1024]{1,0:T(8,128)(2,1)}), bf16[128,512]{1,0:T(8,128)(2,1)}) %reduce-scatter.2.cloned.1.call-update) | async-done | bytes 131088 | tf_op jit(solution)/shard_map/reduce_scatter | solution.py:58
  160.1 1.7 %divide_select_fusion = f32[128,512]{1,0:T(8,128)} fusion(bf16[128,512]{1,0:T(8,128)(2,1)} %reduce-scatter.2.cloned.1.call-done, bf16[128,512]{1,0:T(8,128)(2,1)S(1)} %convolution_convert_fusion.1, f32[128]{0:T(128)S(1)} %multiply_add_fusion, f32[]{:T(128)} %bitcast.8, pred[128]{0:T(512)(128)(4,1)S(1)} %iota_compare_fusion.1), kind=kLoop, calls=%fused_computation.28 | loop fusion | flops 393216 | bytes 524932 | tf_op jit(solution)/shard_map/jit(_where)/select_n | solution.py:66
  (3 shorter events, 0.0 us)
Async XLA Ops:
  7.2 39.4 %copy-start = (bf16[1024,512]{1,0:T(8,128)(2,1)S(1)}, bf16[1024,512]{1,0:T(8,128)(2,1)}, u32[]{:S(2)}) copy-start(bf16[1024,512]{1,0:T(8,128)(2,1)} %param.15) | copy-start | bytes 3145732
  7.2 20.6 %copy-start.1 = (bf16[128,512]{1,0:T(8,128)(2,1)S(1)}, bf16[128,512]{1,0:T(8,128)(2,1)}, u32[]{:S(2)}) copy-start(bf16[128,512]{1,0:T(8,128)(2,1)} %param.10) | copy-start | bytes 393220
  7.2 20.6 %copy-start.5 = (bf16[128,128]{1,0:T(8,128)(2,1)S(1)}, bf16[128,128]{1,0:T(8,128)(2,1)}, u32[]{:S(2)}) copy-start(bf16[128,128]{1,0:T(8,128)(2,1)} %param.11) | copy-start | bytes 98308
  7.2 26.4 %copy-start.6 = (bf16[1024,512]{1,0:T(8,128)(2,1)S(1)}, bf16[1024,512]{1,0:T(8,128)(2,1)}, u32[]{:S(2)}) copy-start(bf16[1024,512]{1,0:T(8,128)(2,1)} %param.13) | copy-start | bytes 3145732
  11.5 15.3 %all-to-all-start = ((bf16[16,8,512]{2,1,0:T(8,128)(2,1)}), bf16[16,8,512]{2,1,0:T(8,128)(2,1)S(1)}, u32[]{:S(2)}, u32[]{:S(2)}) async-start(bf16[16,8,512]{2,1,0:T(8,128)(2,1)} %bitcast_select_fusion), calls=%async_computation | async-start | bytes 262144 | tf_op jit(solution)/shard_map/all_to_all | solution.py:17
  18.9 127.1 %all-reduce.4.cloned.1.call-start = ((), (), s32[]{:S(2)}) async-start(), calls=%async_computation.2 | async-start | bytes 4194304 | tf_op jit(solution)/shard_map/psum | solution.py:52
  33.6 6.6 %copy-start.3 = (bf16[1024,512]{1,0:T(8,128)(2,1)S(1)}, bf16[1024,512]{1,0:T(8,128)(2,1)}, u32[]{:S(2)}) copy-start(bf16[1024,512]{1,0:T(8,128)(2,1)} %param.14) | copy-start | bytes 3145732
  34.5 6.1 %copy-start.4 = (bf16[1024,512]{1,0:T(8,128)(2,1)S(1)}, bf16[1024,512]{1,0:T(8,128)(2,1)}, u32[]{:S(2)}) copy-start(bf16[1024,512]{1,0:T(8,128)(2,1)} %param.16) | copy-start | bytes 3145732
  49.4 110.6 %reduce-scatter.2.cloned.1.call-start = ((), (), s32[]{:S(2)}) async-start(), calls=%async_computation.3 | async-start | bytes 393216 | tf_op jit(solution)/shard_map/reduce_scatter | solution.py:58
  146.1 2.8 %copy-start.2 = (f32[512,1024]{1,0:T(8,128)S(1)}, f32[512,1024]{1,0:T(8,128)}, u32[]{:S(2)}) copy-start(f32[512,1024]{1,0:T(8,128)} %all-reduce.4.cloned.1.call-done) | copy-start | bytes 6291460
Sparse Core Ops, SparseCore 0:
  49.5 96.4 all-reduce.3
  149.0 11.0 reduce-scatter.1
where the time goes:
time: 169 us
  waiting for transfers between devices  75.3 us (45%)
  blocking collectives  51.8 us (31%)
  between operations  16.2 us (10%)
  matrix products  8.33 us (5%)
  starting transfers between devices  7.5 us (4%)
  other arithmetic  6.91 us (4%)
  local copies, waits for them, and re-layouts  2.58 us (2%)
    psum x1, waiting for transfers between devices, local(): lax.psum((key_values, key_total, sq_pair), 'parts')  58.4 us
    psum x1, blocking collectives, local(): lax.psum((key_values, key_total, sq_pair), 'parts')  29.8 us
    reduce_scatter x1, waiting for transfers between devices, local(): lax.psum_scatter(numer_part.astype(jnp.bfloat16), 'mp', scatter_dimension...  9.64 us
    all_to_all x1, starting transfers between devices, local(): lax.all_to_all(outgoing, 'parts', split_axis=0, concat_axis=0, tiled=True)  7.41 us
    all_to_all x1, waiting for transfers between devices, local(): lax.all_to_all(outgoing, 'parts', split_axis=0, concat_axis=0, tiled=True)  7.19 us
    all_gather x1, blocking collectives, local(): portion = lax.all_gather(hidden, 'mp', axis=1, tiled=True)  5.77 us
    all_gather x1, blocking collectives, local(): lax.all_gather(convolved, 'mp', axis=1, tiled=True)  5.64 us
    all_gather x1, blocking collectives, local(): lax.all_gather(values, 'mp', axis=1, tiled=True)  5.64 us
  transfers between devices with their start and end apart: 3, of which 3 were waited for; matrix products, arithmetic and copies ran while one was open for 2% of the time, Pallas kernels for 0%

commit v1 on v0

--- a/solution.py
+++ b/solution.py
@@ -1,12 +1,19 @@
+import functools
 import math
 
 import jax
 import jax.numpy as jnp
 from jax import lax
+from jax.experimental import pallas as pl
+from jax.experimental.pallas import tpu as pltpu
 from jax.sharding import PartitionSpec as P
 
-
-def local(
+MESH = pl.DeviceIdType.MESH
+F32 = jnp.float32
+BF16 = jnp.bfloat16
+
+
+def plain(
     feats, adj_local, adj_halo, w_graph, w_query, w_key, w_value, send_rows, send_count, live
 ):
     row_count, col_count = feats.shape
@@ -66,6 +73,408 @@
     return (jnp.where(live_mask, result, 0.0), key_summary)
 
 
+def dot(a, b):
+    return jnp.dot(a, b, preferred_element_type=F32)
+
+
+def kernel(
+    n,
+    nz,
+    feats,
+    adj_local,
+    adj_halo,
+    send_rows,
+    send_count,
+    live,
+    wg,
+    wq,
+    wk,
+    wv,
+    out,
+    kv_out,
+    wbuf,
+    outgoing,
+    incoming,
+    conv,
+    hid,
+    val,
+    query,
+    key_t,
+    part,
+    send1,
+    recv1,
+    acc2,
+    send2,
+    recv2,
+    send3,
+    recv3,
+    kvb,
+    stat,
+    den,
+    nsend,
+    nrecv,
+    wsem,
+    osem,
+    halo_s,
+    halo_r,
+    mp_s,
+    mp_r,
+    s1_s,
+    s1_r,
+    s2_s,
+    s2_r,
+    s3_s,
+    s3_r,
+    gz_s,
+    gz_r,
+    gy_s,
+    gy_r,
+    gc_s,
+    gc_r,
+    st_s,
+    st_r,
+):
+    p = lax.axis_index("parts")
+    m = lax.axis_index("mp")
+    c, y, z = p % 2, (p // 2) % 2, p // 4
+    other = 1 - m
+    core_peer = p + 1 - 2 * c
+    y_peer = p + 2 - 4 * y
+    rows, cols = feats.shape
+    slots = outgoing.shape[1]
+    half, quarter, piece = cols // 2, cols // 4, cols // n
+    sent = []
+
+    def send(src, dst, s_sem, r_sem, device):
+        copy = pltpu.make_async_remote_copy(
+            src_ref=src,
+            dst_ref=dst,
+            send_sem=s_sem,
+            recv_sem=r_sem,
+            device_id=device,
+            device_id_type=MESH,
+        )
+        copy.start()
+        sent.append(copy)
+        return copy
+
+    loads = []
+    for i, w in enumerate((wg, wv, wk, wq)):
+        load = pltpu.make_async_copy(w, wbuf.at[i], wsem.at[i])
+        load.start()
+        loads.append(load)
+
+    barrier = pltpu.get_barrier_semaphore()
+    for d in range(1, n):
+        pl.semaphore_signal(
+            barrier, inc=1, device_id={"parts": lax.rem(p + d, n)}, device_id_type=MESH
+        )
+    pl.semaphore_signal(barrier, inc=1, device_id={"mp": other}, device_id_type=MESH)
+
+    total = n * slots
+    owner = lax.broadcasted_iota(jnp.int32, (total, n), 0) // slots
+    is_owner = owner == lax.broadcasted_iota(jnp.int32, (total, n), 1)
+    spot = lax.broadcasted_iota(jnp.int32, (total, slots), 0) % slots
+    is_spot = spot == lax.broadcasted_iota(jnp.int32, (total, slots), 1)
+    spread = jnp.dot(
+        is_owner.astype(F32),
+        send_rows[...].astype(F32),
+        precision=lax.Precision.HIGHEST,
+        preferred_element_type=F32,
+    )
+    index = jnp.sum(jnp.where(is_spot, spread, 0.0), axis=1, keepdims=True)
+    count = jnp.sum(
+        jnp.where(is_owner, send_count[...].astype(F32), 0.0), axis=1, keepdims=True
+    )
+    slot_id = jnp.sum(
+        jnp.where(is_spot, lax.broadcasted_iota(jnp.int32, (total, slots), 1), 0).astype(F32),
+        axis=1,
+        keepdims=True,
+    )
+    index = jnp.where(slot_id < count, index, -1.0)
+    node = lax.broadcasted_iota(jnp.int32, (total, rows), 1).astype(F32)
+    pick = jnp.where(index == node, 1.0, 0.0).astype(BF16)
+    outgoing[...] = dot(pick, feats[...]).reshape(n, slots, cols).astype(BF16)
+
+    pl.semaphore_wait(barrier, n)
+    halo = []
+    for d in range(1, n):
+        to = lax.rem(p + d, n)
+        halo.append(
+            send(outgoing.at[to], incoming.at[p], halo_s.at[d], halo_r.at[d], {"parts": to})
+        )
+    incoming[p] = outgoing[p]
+    local_sum = dot(adj_local[...], feats[...])
+    for copy in halo:
+        copy.wait_recv()
+    arrived = incoming[...].astype(F32).reshape(total, cols).astype(BF16)
+    conv[m] = (local_sum + dot(adj_halo[...], arrived)).astype(BF16)
+    swap = send(conv.at[m], conv.at[m], mp_s.at[0], mp_r.at[0], {"mp": other})
+    mine = pl.ds(pl.multiple_of(m * cols, cols), cols)
+    theirs = pl.ds(pl.multiple_of(other * cols, cols), cols)
+    loads[0].wait()
+    projected = dot(conv[m], wbuf[0, mine, :])
+    swap.wait_recv()
+    projected = projected + dot(conv[other], wbuf[0, theirs, :])
+    hid[m] = (0.5 * projected * (1.0 + lax.erf(projected * math.sqrt(0.5)))).astype(BF16)
+    swap = send(hid.at[m], hid.at[m], mp_s.at[1], mp_r.at[1], {"mp": other})
+    for load in loads[1:]:
+        load.wait()
+    own = hid[m]
+    raw_v = dot(own, wbuf[1, mine, :])
+    raw_k = dot(own, wbuf[2, mine, :])
+    raw_q = dot(own, wbuf[3, mine, :])
+    swap.wait_recv()
+    rest = hid[other]
+    val[m] = (raw_v + dot(rest, wbuf[1, theirs, :])).astype(BF16)
+    swap = send(val.at[m], val.at[m], mp_s.at[2], mp_r.at[2], {"mp": other})
+    live_mask = lax.broadcasted_iota(jnp.int32, (rows, 1), 0) < live[0]
+
+    def feature(x):
+        x = jnp.where(x > 0.0, x + 1.0, jnp.exp(jnp.minimum(x, 0.0)))
+        return jnp.where(live_mask, x, 0.0).astype(BF16)
+
+    key_feat = feature(raw_k + dot(rest, wbuf[2, theirs, :]))
+    key_wide = key_feat.astype(F32)
+    key_t[...] = key_wide.T.astype(BF16)
+
+    keep1 = pl.ds(pl.multiple_of(c * half, half), half)
+    give1 = pl.ds(pl.multiple_of((1 - c) * half, half), half)
+    keep2 = pl.ds(pl.multiple_of(y * quarter, quarter), quarter)
+    give2 = pl.ds(pl.multiple_of((1 - y) * quarter, quarter), quarter)
+    step1 = []
+
+    def start1(g, column):
+        part[g] = dot(key_t[...], val[column])
+        send1[g] = part[g, give1, :].astype(BF16)
+        step1.append(
+            send(send1.at[g], recv1.at[g], s1_s.at[g], s1_r.at[g], {"parts": core_peer})
+        )
+
+    start1(0, m)
+    query[...] = feature(raw_q + dot(rest, wbuf[3, theirs, :]))
+    query_wide = query[...].astype(F32)
+    lane = lax.broadcasted_iota(jnp.int32, (1, 128), 1)
+    query_sq = jnp.sum(jnp.sum(query_wide * query_wide, axis=0, keepdims=True), axis=1, keepdims=True)
+    key_sq = jnp.sum(jnp.sum(key_wide * key_wide, axis=0, keepdims=True), axis=1, keepdims=True)
+    stat[0, :, :cols] = jnp.sum(key_wide, axis=0, keepdims=True)
+    stat[0, :, cols:] = jnp.where(lane == 0, query_sq, jnp.where(lane == 1, key_sq, 0.0))
+    swap.wait_recv()
+    start1(1, other)
+    stats = []
+    for d in range(1, n):
+        stats.append(
+            send(stat.at[0], stat.at[d], st_s.at[d], st_r.at[d], {"parts": lax.rem(p + d, n)})
+        )
+    step2 = []
+    for g in range(2):
+        step1[g].wait_recv()
+        send2[g] = (
+            part[g, pl.ds(pl.multiple_of(c * half + (1 - y) * quarter, quarter), quarter), :]
+            + recv1[g, give2, :].astype(F32)
+        ).astype(BF16)
+        step2.append(
+            send(send2.at[g], recv2.at[g], s2_s.at[g], s2_r.at[g], {"parts": y_peer})
+        )
+        acc2[g] = part[
+            g, pl.ds(pl.multiple_of(c * half + y * quarter, quarter), quarter), :
+        ] + recv1[g, keep2, :].astype(F32)
+    step3 = []
+    for g in range(2):
+        step2[g].wait_recv()
+        acc2[g] = acc2[g] + recv2[g].astype(F32)
+        send3[g] = acc2[g].astype(BF16)
+        for d in range(1, nz):
+            to = lax.rem(z + d, nz)
+            step3.append(
+                send(
+                    send3.at[g, pl.ds(pl.multiple_of(to * piece, piece), piece), :],
+                    recv3.at[g, d],
+                    s3_s.at[g, d],
+                    s3_r.at[g, d],
+                    {"parts": to * 4 + p % 4},
+                )
+            )
+
+    def block(zz):
+        return pl.ds(pl.multiple_of(c * half + y * quarter + zz * piece, piece), piece)
+
+    gather_z, gather_y, gather_c = [], [], []
+
+    def pass_on(g, column, d):
+        place = kvb.at[column, block(lax.rem(z + nz - d, nz)), :]
+        gather_y.append(send(place, place, gy_s.at[g, d], gy_r.at[g, d], {"parts": y_peer}))
+
+    for g, column in enumerate((m, other)):
+        final = acc2[g, pl.ds(pl.multiple_of(z * piece, piece), piece), :]
+        for d in range(1, nz):
+            step3[g * (nz - 1) + d - 1].wait_recv()
+            final = final + recv3[g, d].astype(F32)
+        kvb[column, block(z), :] = final.astype(BF16)
+        place = kvb.at[column, block(z), :]
+        for d in range(1, nz):
+            gather_z.append(
+                send(
+                    place,
+                    place,
+                    gz_s.at[g, d],
+                    gz_r.at[g, d],
+                    {"parts": lax.rem(z + d, nz) * 4 + p % 4},
+                )
+            )
+        pass_on(g, column, 0)
+
+    for copy in stats:
+        copy.wait_recv()
+    sums = stat[0]
+    for d in range(1, n):
+        sums = sums + stat[d]
+    den[m, :rows, :] = jnp.broadcast_to(
+        jnp.sum(query_wide * sums[:, :cols], axis=1, keepdims=True), (rows, 128)
+    )
+    den[m, rows:, :] = jnp.broadcast_to(sums[:, cols:], (8, 128))
+    den_swap = send(den.at[m], den.at[m], mp_s.at[3], mp_r.at[3], {"mp": other})
+
+    def keep_block(column, yy):
+        return kvb.at[
+            column, pl.ds(pl.multiple_of(c * half + yy * quarter, quarter), quarter), :
+        ]
+
+    for g, column in enumerate((m, other)):
+        for d in range(1, nz):
+            gather_z[g * (nz - 1) + d - 1].wait_recv()
+            pass_on(g, column, d)
+        place = keep_block(column, y)
+        gather_c.append(send(place, place, gc_s.at[g, 0], gc_r.at[g, 0], {"parts": core_peer}))
+    for g, column in enumerate((m, other)):
+        gather_y[g].wait_recv()
+        for d in range(1, nz):
+            gather_y[2 + g * (nz - 1) + d - 1].wait_recv()
+        place = keep_block(column, 1 - y)
+        gather_c.append(send(place, place, gc_s.at[g, 1], gc_r.at[g, 1], {"parts": core_peer}))
+    gather_c[0].wait_recv()
+    gather_c[2].wait_recv()
+    numerator = dot(query[...], kvb[m])
+    gather_c[1].wait_recv()
+    gather_c[3].wait_recv()
+    nsend[...] = dot(query[...], kvb[other]).astype(BF16)
+    swap = send(nsend, nrecv, mp_s.at[4], mp_r.at[4], {"mp": other})
+    stores = []
+    for g in range(2):
+        store = pltpu.make_async_copy(kvb.at[g], kv_out.at[:, pl.ds(g * cols, cols)], osem.at[g])
+        store.start()
+        stores.append(store)
+    den_swap.wait_recv()
+    square = den[0, rows : rows + 1, :] + den[1, rows : rows + 1, :]
+    query_sq = jnp.sum(jnp.where(lane == 0, square, 0.0), axis=1, keepdims=True)
+    key_sq = jnp.sum(jnp.where(lane == 1, square, 0.0), axis=1, keepdims=True)
+    inverse = lax.rsqrt(query_sq) * lax.rsqrt(key_sq)
+    denominator = den[0, :rows, 0:1] + den[1, :rows, 0:1]
+    scale = 1.0 + denominator * inverse
+    swap.wait_recv()
+    numerator = numerator + nrecv[...].astype(F32)
+    result = (val[m].astype(F32) + numerator * inverse) / scale
+    out[...] = jnp.where(live_mask, result, 0.0)
+    for store in stores:
+        store.wait()
+    for copy in sent:
+        copy.wait_send()
+
+
+def fused(
+    feats, adj_local, adj_halo, w_graph, w_query, w_key, w_value, send_rows, send_count, live
+):
+    n = lax.axis_size("parts")
+    nz = n // 4
+    rows, cols = feats.shape
+    slots = send_rows.shape[2]
+    depth = w_graph.shape[0]
+    half, quarter, piece = cols // 2, cols // 4, cols // n
+    vmem = pl.BlockSpec(memory_space=pltpu.VMEM)
+    hbm = pl.BlockSpec(memory_space=pl.ANY)
+    dma = pltpu.SemaphoreType.DMA
+    out, kv = pl.pallas_call(
+        functools.partial(kernel, n, nz),
+        out_shape=(
+            jax.ShapeDtypeStruct((rows, cols), F32),
+            jax.ShapeDtypeStruct((cols, depth), BF16),
+        ),
+        in_specs=[vmem] * 5 + [pl.BlockSpec(memory_space=pltpu.SMEM)] + [hbm] * 4,
+        out_specs=(vmem, hbm),
+        scratch_shapes=[
+            pltpu.VMEM((4, depth, cols), BF16),
+            pltpu.VMEM((n, slots, cols), BF16),
+            pltpu.VMEM((n, slots, cols), BF16),
+            pltpu.VMEM((2, rows, cols), BF16),
+            pltpu.VMEM((2, rows, cols), BF16),
+            pltpu.VMEM((2, rows, cols), BF16),
+            pltpu.VMEM((rows, cols), BF16),
+            pltpu.VMEM((cols, rows), BF16),
+            pltpu.VMEM((2, cols, cols), F32),
+            pltpu.VMEM((2, half, cols), BF16),
+            pltpu.VMEM((2, half, cols), BF16),
+            pltpu.VMEM((2, quarter, cols), F32),
+            pltpu.VMEM((2, quarter, cols), BF16),
+            pltpu.VMEM((2, quarter, cols), BF16),
+            pltpu.VMEM((2, quarter, cols), BF16),
+            pltpu.VMEM((2, nz, piece, cols), BF16),
+            pltpu.VMEM((2, cols, cols), BF16),
+            pltpu.VMEM((n, 1, cols + 128), F32),
+            pltpu.VMEM((2, rows + 8, 128), F32),
+            pltpu.VMEM((rows, cols), BF16),
+            pltpu.VMEM((rows, cols), BF16),
+            dma((4,)),
+            dma((2,)),
+            dma((n,)),
+            dma((n,)),
+            dma((5,)),
+            dma((5,)),
+            dma((2,)),
+            dma((2,)),
+            dma((2,)),
+            dma((2,)),
+            dma((2, nz)),
+            dma((2, nz)),
+            dma((2, nz)),
+            dma((2, nz)),
+            dma((2, nz)),
+            dma((2, nz)),
+            dma((2, 2)),
+            dma((2, 2)),
+            dma((n,)),
+            dma((n,)),
+        ],
+        compiler_params=pltpu.CompilerParams(collective_id=0, has_side_effects=True),
+    )(
+        feats,
+        adj_local,
+        adj_halo,
+        send_rows[0],
+        send_count,
+        live,
+        w_graph,
+        w_query,
+        w_key,
+        w_value,
+    )
+    return out, kv.astype(F32) / math.sqrt(n * rows)
+
+
+def local(*args):
+    n = lax.axis_size("parts")
+    rows, cols = args[0].shape
+    slots = args[7].shape[2]
+    fits = (
+        lax.axis_size("mp") == 2
+        and n % 4 == 0
+        and cols % (16 * n) == 0
+        and rows % 16 == 0
+        and (n * slots) % 16 == 0
+        and slots % 8 == 0
+    )
+    return fused(*args) if fits else plain(*args)
+
+
 def solution(mesh):
     return jax.shard_map(
         local,

time: 169 us -> 59.7 us (0.35)
  waiting for transfers between devices: 75.3 us -> 0 us
  Pallas kernels: 0 us -> 53.2 us
  blocking collectives: 51.8 us -> 0 us
  between operations: 16.2 us -> 1.29 us
  matrix products: 8.33 us -> 0 us
  starting transfers between devices: 7.5 us -> 0 us
  other arithmetic: 6.91 us -> 2.87 us
    psum x1 -> x0, waiting for transfers between devices: 58.4 us -> none  [local(): lax.psum((key_values, key_total, sq_pair), 'parts')]
    pallas_call x0 -> x1, Pallas kernels: none -> 53.2 us  [fused(): pl.pallas_call(functools.partial(kernel, n, nz), out_shape=(jax.ShapeDtyp...]
    psum x2 -> x0, blocking collectives: 34.7 us -> none  [the longest x1 29.8 us: local(): lax.psum((key_values, key_total, sq_pair), 'parts')]
    all_gather x3 -> x0, blocking collectives: 17 us -> none  [the longest x1 5.77 us: local(): portion = lax.all_gather(hidden, 'mp', axis=1, tiled=True)]
    reduce_scatter x1 -> x0, waiting for transfers between devices: 9.64 us -> none  [local(): lax.psum_scatter(numer_part.astype(jnp.bfloat16), 'mp', scatter_dimension...]
    dot_general x9 -> x0, matrix products: 8.33 us -> none  [the longest x1 2.75 us: local(): jnp.dot(query_feat, key_values.astype(jnp.bfloat16), preferred_element_ty...]
    all_to_all x1 -> x0, starting transfers between devices: 7.41 us -> none  [local(): lax.all_to_all(outgoing, 'parts', split_axis=0, concat_axis=0, tiled=True)]
    all_to_all x1 -> x0, waiting for transfers between devices: 7.19 us -> none  [local(): lax.all_to_all(outgoing, 'parts', split_axis=0, concat_axis=0, tiled=True)]
  transfers between devices with their start and end apart: 3 -> 0, of which waited for: 3 -> 0; matrix products, arithmetic and copies ran while one was open for 2% -> 0% of each run, Pallas kernels for 0% -> 0%
where the time goes in v1:
time: 59.7 us; the launch traced here: 59.5 us
  Pallas kernels  53.2 us (89%)
  other arithmetic  2.87 us (5%)
  local copies, waits for them, and re-layouts  2.06 us (3%)
  between operations  1.29 us (2%)
    pallas_call x1, Pallas kernels, fused(): pl.pallas_call(functools.partial(kernel, n, nz), out_shape=(jax.ShapeDtyp...  53.2 us
    div x1, other arithmetic, fused(): return (out, kv.astype(F32) / math.sqrt(n * rows))  2.87 us
    squeeze x1, local copies, waits for them, and re-layouts, fused(): send_rows[0]  1.36 us

profile of v1, /device:TPU:0, one launch (start us, length us, event | category | flops | bytes accessed | tf_op | source)
XLA Modules:
  0.0 59.5 jit_solution(11195109967644994614)
XLA Ops:
  1.3 1.4 %copy.12.send_rows = s32[16,8]{1,0:T(8,128)} copy(s32[16,8]{0,1:T(8,128)} %bitcast.1) | data formatting | bytes 1024 | tf_op jit(solution)/shard_map/squeeze | solution.py:452
  2.6 53.2 %shard_map.113 = (f32[128,512]{1,0:T(8,128)}, bf16[512,1024]{1,0:T(8,128)(2,1)}) custom-call(bf16[128,512]{1,0:T(8,128)(2,1)} %feats.1, bf16[128,128]{1,0:T(8,128)(2,1)} %adj_local.1, bf16[128,128]{1,0:T(8,128)(2,1)} %adj_halo.1, s32[16,8]{1,0:T(8,128)} %copy.12.send_rows, s32[1,16]{1,0:T(1,128)} %send_count.1, s32[1]{0:T(128)S(6)} %copy.14.live, ...), custom_call_target="tpu_custom_call" | custom-call | tf_op jit(solution)/shard_map/pallas_call | solution.py:396
  55.9 0.0 copy-start
  55.9 2.9 %convert_multiply_fusion = f32[512,1024]{1,0:T(8,128)} fusion(bf16[512,1024]{1,0:T(8,128)(2,1)} %get-tuple-element.5), kind=kLoop, calls=%fused_computation | loop fusion | flops 1048576 | bytes 3145728 | tf_op jit(solution)/shard_map/div | solution.py:460
  58.7 0.0 copy-done
  58.7 0.7 %copy.15 = f32[128,512]{1,0:T(8,128)} copy(f32[128,512]{1,0:T(8,128)S(1)} %copy-done) | data formatting | bytes 524288
Async XLA Ops:
  55.9 2.9 %copy-start = (f32[128,512]{1,0:T(8,128)S(1)}, f32[128,512]{1,0:T(8,128)}, u32[]{:S(2)}) copy-start(f32[128,512]{1,0:T(8,128)} %get-tuple-element.8) | copy-start | bytes 786436

commit v2 on v1

--- a/solution.py
+++ b/solution.py
@@ -80,11 +80,11 @@
 def kernel(
     n,
     nz,
-    feats,
-    adj_local,
-    adj_halo,
-    send_rows,
-    send_count,
+    feats_in,
+    adj_local_in,
+    adj_halo_in,
+    send_rows_in,
+    send_count_in,
     live,
     wg,
     wq,
@@ -92,6 +92,11 @@
     wv,
     out,
     kv_out,
+    feats,
+    adj_local,
+    adj_halo,
+    send_rows,
+    send_count,
     wbuf,
     outgoing,
     incoming,
@@ -113,6 +118,7 @@
     den,
     nsend,
     nrecv,
+    isem,
     wsem,
     osem,
     halo_s,
@@ -158,6 +164,19 @@
         sent.append(copy)
         return copy
 
+    inputs = []
+    for i, (source, place) in enumerate(
+        (
+            (send_rows_in, send_rows),
+            (send_count_in, send_count),
+            (feats_in, feats),
+            (adj_local_in, adj_local),
+            (adj_halo_in, adj_halo),
+        )
+    ):
+        load = pltpu.make_async_copy(source, place, isem.at[i])
+        load.start()
+        inputs.append(load)
     loads = []
     for i, w in enumerate((wg, wv, wk, wq)):
         load = pltpu.make_async_copy(w, wbuf.at[i], wsem.at[i])
@@ -171,14 +190,18 @@
         )
     pl.semaphore_signal(barrier, inc=1, device_id={"mp": other}, device_id_type=MESH)
 
+    for load in inputs:
+        load.wait()
+
     total = n * slots
     owner = lax.broadcasted_iota(jnp.int32, (total, n), 0) // slots
     is_owner = owner == lax.broadcasted_iota(jnp.int32, (total, n), 1)
     spot = lax.broadcasted_iota(jnp.int32, (total, slots), 0) % slots
     is_spot = spot == lax.broadcasted_iota(jnp.int32, (total, slots), 1)
-    spread = jnp.dot(
+    spread = lax.dot_general(
         is_owner.astype(F32),
         send_rows[...].astype(F32),
+        (((1,), (1,)), ((), ())),
         precision=lax.Precision.HIGHEST,
         preferred_element_type=F32,
     )
@@ -245,11 +268,11 @@
     step1 = []
 
     def start1(g, column):
-        part[g] = dot(key_t[...], val[column])
-        send1[g] = part[g, give1, :].astype(BF16)
+        send1[g] = dot(key_t[give1, :], val[column]).astype(BF16)
         step1.append(
             send(send1.at[g], recv1.at[g], s1_s.at[g], s1_r.at[g], {"parts": core_peer})
         )
+        part[g] = dot(key_t[keep1, :], val[column])
 
     start1(0, m)
     query[...] = feature(raw_q + dot(rest, wbuf[3, theirs, :]))
@@ -270,15 +293,13 @@
     for g in range(2):
         step1[g].wait_recv()
         send2[g] = (
-            part[g, pl.ds(pl.multiple_of(c * half + (1 - y) * quarter, quarter), quarter), :]
+            part[g, give2, :]
             + recv1[g, give2, :].astype(F32)
         ).astype(BF16)
         step2.append(
             send(send2.at[g], recv2.at[g], s2_s.at[g], s2_r.at[g], {"parts": y_peer})
         )
-        acc2[g] = part[
-            g, pl.ds(pl.multiple_of(c * half + y * quarter, quarter), quarter), :
-        ] + recv1[g, keep2, :].astype(F32)
+        acc2[g] = part[g, keep2, :] + recv1[g, keep2, :].astype(F32)
     step3 = []
     for g in range(2):
         step2[g].wait_recv()
@@ -391,17 +412,23 @@
     depth = w_graph.shape[0]
     half, quarter, piece = cols // 2, cols // 4, cols // n
     vmem = pl.BlockSpec(memory_space=pltpu.VMEM)
-    hbm = pl.BlockSpec(memory_space=pl.ANY)
+    hbm = pl.BlockSpec(memory_space=pltpu.HBM)
     dma = pltpu.SemaphoreType.DMA
+    place = functools.partial(pltpu.with_memory_space_constraint, memory_space=pltpu.HBM)
     out, kv = pl.pallas_call(
         functools.partial(kernel, n, nz),
         out_shape=(
             jax.ShapeDtypeStruct((rows, cols), F32),
             jax.ShapeDtypeStruct((cols, depth), BF16),
         ),
-        in_specs=[vmem] * 5 + [pl.BlockSpec(memory_space=pltpu.SMEM)] + [hbm] * 4,
-        out_specs=(vmem, hbm),
+        in_specs=[hbm] * 5 + [pl.BlockSpec(memory_space=pltpu.SMEM)] + [hbm] * 4,
+        out_specs=(vmem, pl.BlockSpec(memory_space=pl.ANY)),
         scratch_shapes=[
+            pltpu.VMEM(feats.shape, BF16),
+            pltpu.VMEM(adj_local.shape, BF16),
+            pltpu.VMEM(adj_halo.shape, BF16),
+            pltpu.VMEM((slots, n), jnp.int32),
+            pltpu.VMEM((1, n), jnp.int32),
             pltpu.VMEM((4, depth, cols), BF16),
             pltpu.VMEM((n, slots, cols), BF16),
             pltpu.VMEM((n, slots, cols), BF16),
@@ -410,7 +437,7 @@
             pltpu.VMEM((2, rows, cols), BF16),
             pltpu.VMEM((rows, cols), BF16),
             pltpu.VMEM((cols, rows), BF16),
-            pltpu.VMEM((2, cols, cols), F32),
+            pltpu.VMEM((2, half, cols), F32),
             pltpu.VMEM((2, half, cols), BF16),
             pltpu.VMEM((2, half, cols), BF16),
             pltpu.VMEM((2, quarter, cols), F32),
@@ -423,6 +450,7 @@
             pltpu.VMEM((2, rows + 8, 128), F32),
             pltpu.VMEM((rows, cols), BF16),
             pltpu.VMEM((rows, cols), BF16),
+            dma((5,)),
             dma((4,)),
             dma((2,)),
             dma((n,)),
@@ -444,18 +472,13 @@
             dma((n,)),
             dma((n,)),
         ],
-        compiler_params=pltpu.CompilerParams(collective_id=0, has_side_effects=True),
+        compiler_params=pltpu.CompilerParams(
+            collective_id=0, has_side_effects=True, vmem_limit_bytes=24 * 1024 * 1024
+        ),
     )(
-        feats,
-        adj_local,
-        adj_halo,
-        send_rows[0],
-        send_count,
+        *(place(a) for a in (feats, adj_local, adj_halo, send_rows[0].T, send_count)),
         live,
-        w_graph,
-        w_query,
-        w_key,
-        w_value,
+        *(place(w) for w in (w_graph, w_query, w_key, w_value)),
     )
     return out, kv.astype(F32) / math.sqrt(n * rows)
 

time: 59.7 us -> 55.8 us (0.935)
  local copies, waits for them, and re-layouts: 2.06 us -> 0.7 us
  other arithmetic: 2.87 us -> 1.6 us
  Pallas kernels: 53.2 us -> 52 us
    squeeze x1 -> x0, local copies, waits for them, and re-layouts: 1.36 us -> none  [fused(): send_rows[0]]
    div x1, other arithmetic: 2.87 us -> 1.6 us  [fused(): return (out, kv.astype(F32) / math.sqrt(n * rows))]
    pallas_call x1, Pallas kernels: 53.2 us -> 52 us  [fused(): pl.pallas_call(functools.partial(kernel, n, nz), out_shape=(jax.ShapeDtyp...]
where the time goes in v2:
time: 55.8 us; the launch traced here: 55.6 us
  Pallas kernels  52 us (93%)
  other arithmetic  1.6 us (3%)
  between operations  1.29 us (2%)
  local copies, waits for them, and re-layouts  0.7 us (1%)
    pallas_call x1, Pallas kernels, fused(): pl.pallas_call(functools.partial(kernel, n, nz), out_shape=(jax.ShapeDtyp...  52 us
    div x1, other arithmetic, fused(): return (out, kv.astype(F32) / math.sqrt(n * rows))  1.6 us

profile of v2, /device:TPU:0, one launch (start us, length us, event | category | flops | bytes accessed | tf_op | source)
XLA Modules:
  0.0 55.6 jit_solution(11025766331231262409)
XLA Ops:
  1.3 52.0 %shard_map.113 = (f32[128,512]{1,0:T(8,128)S(1)}, bf16[512,1024]{1,0:T(8,128)(2,1)S(1)}) custom-call(bf16[128,512]{1,0:T(8,128)(2,1)} %feats_in.1, bf16[128,128]{1,0:T(8,128)(2,1)} %adj_local_in.1, bf16[128,128]{1,0:T(8,128)(2,1)} %adj_halo_in.1, s32[8,16]{1,0:T(8,128)} %bitcast.3, s32[1,16]{1,0:T(1,128)} %send_count_in.1, s32[1]{0:T(128)S(6)} %copy.13.live, ...), custom_call_target="tpu_custom_call" | custom-call | tf_op jit(solution)/shard_map/pallas_call | solution.py:418
  53.3 1.6 %convert_multiply_fusion = f32[512,1024]{1,0:T(8,128)} fusion(bf16[512,1024]{1,0:T(8,128)(2,1)S(1)} %get-tuple-element.5), kind=kLoop, calls=%fused_computation | loop fusion | flops 1048576 | bytes 3145728 | tf_op jit(solution)/shard_map/div | solution.py:483
  54.9 0.7 %copy.14 = f32[128,512]{1,0:T(8,128)} copy(f32[128,512]{1,0:T(8,128)S(1)} %get-tuple-element.8) | data formatting | bytes 524288

commit v3 on v2

--- a/solution.py
+++ b/solution.py
@@ -289,59 +289,62 @@
         stats.append(
             send(stat.at[0], stat.at[d], st_s.at[d], st_r.at[d], {"parts": lax.rem(p + d, n)})
         )
-    step2 = []
-    for g in range(2):
+    step2, step3 = {}, {}
+    order = ((1, other), (0, m))
+    for g, _ in order:
         step1[g].wait_recv()
         send2[g] = (
             part[g, give2, :]
             + recv1[g, give2, :].astype(F32)
         ).astype(BF16)
-        step2.append(
-            send(send2.at[g], recv2.at[g], s2_s.at[g], s2_r.at[g], {"parts": y_peer})
+        step2[g] = send(
+            send2.at[g], recv2.at[g], s2_s.at[g], s2_r.at[g], {"parts": y_peer}
         )
         acc2[g] = part[g, keep2, :] + recv1[g, keep2, :].astype(F32)
-    step3 = []
-    for g in range(2):
+    for g, _ in order:
         step2[g].wait_recv()
         acc2[g] = acc2[g] + recv2[g].astype(F32)
         send3[g] = acc2[g].astype(BF16)
         for d in range(1, nz):
             to = lax.rem(z + d, nz)
-            step3.append(
-                send(
-                    send3.at[g, pl.ds(pl.multiple_of(to * piece, piece), piece), :],
-                    recv3.at[g, d],
-                    s3_s.at[g, d],
-                    s3_r.at[g, d],
-                    {"parts": to * 4 + p % 4},
-                )
+            step3[g, d] = send(
+                send3.at[g, pl.ds(pl.multiple_of(to * piece, piece), piece), :],
+                recv3.at[g, d],
+                s3_s.at[g, d],
+                s3_r.at[g, d],
+                {"parts": to * 4 + p % 4},
             )
 
-    def block(zz):
-        return pl.ds(pl.multiple_of(c * half + y * quarter + zz * piece, piece), piece)
-
-    gather_z, gather_y, gather_c = [], [], []
+    def block(column, yy, zz):
+        first = c * half + yy * quarter + zz * piece
+        return kvb.at[column, pl.ds(pl.multiple_of(first, piece), piece), :]
+
+    gather_z, gather_y, gather_c = {}, {}, {}
+
+    def to_core(g, place, i):
+        gather_c[g, i] = send(
+            place, place, gc_s.at[g, i], gc_r.at[g, i], {"parts": core_peer}
+        )
 
     def pass_on(g, column, d):
-        place = kvb.at[column, block(lax.rem(z + nz - d, nz)), :]
-        gather_y.append(send(place, place, gy_s.at[g, d], gy_r.at[g, d], {"parts": y_peer}))
-
-    for g, column in enumerate((m, other)):
+        place = block(column, y, lax.rem(z + nz - d, nz))
+        gather_y[g, d] = send(place, place, gy_s.at[g, d], gy_r.at[g, d], {"parts": y_peer})
+        to_core(g, place, d)
+
+    for g, column in order:
         final = acc2[g, pl.ds(pl.multiple_of(z * piece, piece), piece), :]
         for d in range(1, nz):
-            step3[g * (nz - 1) + d - 1].wait_recv()
+            step3[g, d].wait_recv()
             final = final + recv3[g, d].astype(F32)
-        kvb[column, block(z), :] = final.astype(BF16)
-        place = kvb.at[column, block(z), :]
+        place = block(column, y, z)
+        place[...] = final.astype(BF16)
         for d in range(1, nz):
-            gather_z.append(
-                send(
-                    place,
-                    place,
-                    gz_s.at[g, d],
-                    gz_r.at[g, d],
-                    {"parts": lax.rem(z + d, nz) * 4 + p % 4},
-                )
+            gather_z[g, d] = send(
+                place,
+                place,
+                gz_s.at[g, d],
+                gz_r.at[g, d],
+                {"parts": lax.rem(z + d, nz) * 4 + p % 4},
             )
         pass_on(g, column, 0)
 
@@ -356,30 +359,23 @@
     den[m, rows:, :] = jnp.broadcast_to(sums[:, cols:], (8, 128))
     den_swap = send(den.at[m], den.at[m], mp_s.at[3], mp_r.at[3], {"mp": other})
 
-    def keep_block(column, yy):
-        return kvb.at[
-            column, pl.ds(pl.multiple_of(c * half + yy * quarter, quarter), quarter), :
-        ]
-
-    for g, column in enumerate((m, other)):
+    for g, column in order:
         for d in range(1, nz):
-            gather_z[g * (nz - 1) + d - 1].wait_recv()
+            gather_z[g, d].wait_recv()
             pass_on(g, column, d)
-        place = keep_block(column, y)
-        gather_c.append(send(place, place, gc_s.at[g, 0], gc_r.at[g, 0], {"parts": core_peer}))
-    for g, column in enumerate((m, other)):
-        gather_y[g].wait_recv()
-        for d in range(1, nz):
-            gather_y[2 + g * (nz - 1) + d - 1].wait_recv()
-        place = keep_block(column, 1 - y)
-        gather_c.append(send(place, place, gc_s.at[g, 1], gc_r.at[g, 1], {"parts": core_peer}))
-    gather_c[0].wait_recv()
-    gather_c[2].wait_recv()
-    numerator = dot(query[...], kvb[m])
-    gather_c[1].wait_recv()
-    gather_c[3].wait_recv()
-    nsend[...] = dot(query[...], kvb[other]).astype(BF16)
-    swap = send(nsend, nrecv, mp_s.at[4], mp_r.at[4], {"mp": other})
+
+    numerators = []
+    for g, column in order:
+        for d in range(nz):
+            gather_y[g, d].wait_recv()
+            to_core(g, block(column, 1 - y, lax.rem(z + nz - d, nz)), nz + d)
+        for i in range(2 * nz):
+            gather_c[g, i].wait_recv()
+        numerators.append(dot(query[...], kvb[column]))
+        if g == 1:
+            nsend[...] = numerators[0].astype(BF16)
+            swap = send(nsend, nrecv, mp_s.at[4], mp_r.at[4], {"mp": other})
+    numerator = numerators[1]
     stores = []
     for g in range(2):
         store = pltpu.make_async_copy(kvb.at[g], kv_out.at[:, pl.ds(g * cols, cols)], osem.at[g])
@@ -467,8 +463,8 @@
             dma((2, nz)),
             dma((2, nz)),
             dma((2, nz)),
-            dma((2, 2)),
-            dma((2, 2)),
+            dma((2, 2 * nz)),
+            dma((2, 2 * nz)),
             dma((n,)),
             dma((n,)),
         ],

time: 55.8 us -> 55.8 us (level)
  no operation moved by 1% of the time
where the time goes in v3:
time: 55.8 us; the launch traced here: 55.6 us
  Pallas kernels  52 us (93%)
  other arithmetic  1.6 us (3%)
  between operations  1.29 us (2%)
  local copies, waits for them, and re-layouts  0.7 us (1%)
    pallas_call x1, Pallas kernels, fused(): pl.pallas_call(functools.partial(kernel, n, nz), out_shape=(jax.ShapeDtyp...  52 us
    div x1, other arithmetic, fused(): return (out, kv.astype(F32) / math.sqrt(n * rows))  1.6 us

profile of v3, /device:TPU:0, one launch (start us, length us, event | category | flops | bytes accessed | tf_op | source)
XLA Modules:
  0.0 55.6 jit_solution(13114961199826640376)
XLA Ops:
  1.3 52.0 %shard_map.113 = (f32[128,512]{1,0:T(8,128)S(1)}, bf16[512,1024]{1,0:T(8,128)(2,1)S(1)}) custom-call(bf16[128,512]{1,0:T(8,128)(2,1)} %feats_in.1, bf16[128,128]{1,0:T(8,128)(2,1)} %adj_local_in.1, bf16[128,128]{1,0:T(8,128)(2,1)} %adj_halo_in.1, s32[8,16]{1,0:T(8,128)} %bitcast.3, s32[1,16]{1,0:T(1,128)} %send_count_in.1, s32[1]{0:T(128)S(6)} %copy.13.live, ...), custom_call_target="tpu_custom_call" | custom-call | tf_op jit(solution)/shard_map/pallas_call | solution.py:414
  53.3 1.6 %convert_multiply_fusion = f32[512,1024]{1,0:T(8,128)} fusion(bf16[512,1024]{1,0:T(8,128)(2,1)S(1)} %get-tuple-element.5), kind=kLoop, calls=%fused_computation | loop fusion | flops 1048576 | bytes 3145728 | tf_op jit(solution)/shard_map/div | solution.py:479
  54.9 0.7 %copy.14 = f32[128,512]{1,0:T(8,128)} copy(f32[128,512]{1,0:T(8,128)S(1)} %get-tuple-element.8) | data formatting | bytes 524288
